TPU v7x, 32 devices: a whole 2x2x4 slice. The times are simulated.
32 devices in a mesh: blk: 8 (over z, y), rep: 4 (over x, core).
Axes of the slice: x: 2, y: 2, z: 4, core: 2. Of those that a mesh axis runs over, the one named last changes fastest.
Arguments:
- features: bfloat16 [8192, 256], P(('blk', 'rep')), may hold values from -6 to 6
- tiles: bfloat16 [8, 64, 128, 128], P('blk', 'rep'), may hold values from -0.25 to 0.25
- tile_rows: int32 [8, 64], P('blk', 'rep'), may hold values from 0 to 7
- tile_cols: int32 [8, 64], P('blk', 'rep'), may hold values from 0 to 15
- counts: int32 [8, 4], P('blk', 'rep'), may hold values from 4 to 16
- weight: bfloat16 [256, 256], replicated, may hold values from -0.375 to 0.375
- bias: float32 [256], replicated, may hold values from -3 to 3
- cotangent: bfloat16 [8192, 256], P(('blk', 'rep')), may hold values from -6 to 6
Outputs:
- activations: bfloat16 [8192, 256], P(('blk', 'rep'))
- feature_grad: bfloat16 [8192, 256], P(('blk', 'rep'))
- weight_grad: float32 [256, 256], replicated
- bias_grad: float32 [256], replicated
All inputs are finite; a program needn't handle non-finite values.
Results may differ from a plain program's by a relative error of at most 0.006.
Values may be sent and summed in bfloat16 or wider, within the bound.
A program may use at most 64 MiB of HBM per device.

v0:
```python
import jax
import jax.numpy as jnp
from jax import lax
from jax.sharding import PartitionSpec as P


def shifted(block, axis, distance):
    devices = range(lax.axis_size(axis))
    route = [((i - distance) % len(devices), i) for i in devices]
    return lax.ppermute(block, axis, route)


def per_device(features, tiles, tile_rows, tile_cols, counts, weight, bias, cotangent):
    highest = lax.Precision.HIGHEST
    tile_size = tiles.shape[2]
    slot_count = tiles.shape[1]
    feat_width = features.shape[1]
    own_rows = features.shape[0]
    own_tiles = own_rows // tile_size
    rep_count = lax.axis_size("rep")
    blk_count = lax.axis_size("blk")
    slot_tiles = tiles[0]
    row_index = tile_rows[0]
    col_index = tile_cols[0]
    slot_live = (jnp.arange(slot_count, dtype=jnp.int32) < counts[0, 0]).astype(jnp.float32)
    wanted = col_index[:, None] * tile_size + jnp.arange(tile_size, dtype=jnp.int32)[None, :]
    piece = lax.all_gather(features, "blk", axis=0, tiled=True)
    piece_count = piece.shape[0]
    inside = (wanted >= 0) & (wanted < piece_count)
    clipped = jnp.clip(wanted, 0, piece_count - 1)
    taken = jnp.take(piece, clipped.reshape(-1), axis=0).reshape(slot_count, tile_size, feat_width)
    selected = jnp.where(inside[:, :, None], taken, jnp.zeros((), jnp.bfloat16))
    partial_value = jnp.einsum(
        "sij,sjf->sif", slot_tiles, selected, preferred_element_type=jnp.float32
    )
    row_onehot = (
        row_index[:, None] == jnp.arange(rep_count * own_tiles, dtype=jnp.int32)[None, :]
    ).astype(jnp.float32) * slot_live[:, None]
    summed = jnp.einsum("st,sif->tif", row_onehot, partial_value, precision=highest)
    aggregate = lax.psum_scatter(
        summed.reshape(rep_count * own_rows, feat_width), "rep", scatter_dimension=0, tiled=True
    ).astype(jnp.bfloat16)
    pre_act = jnp.dot(aggregate, weight, preferred_element_type=jnp.float32) + bias[None, :]
    logistic = jax.nn.sigmoid(pre_act)
    activations = (pre_act * logistic).astype(jnp.bfloat16)
    act_grad = (
        cotangent.astype(jnp.float32) * logistic * (1.0 + pre_act * (1.0 - logistic))
    ).astype(jnp.bfloat16)
    local_weight = jnp.dot(aggregate.T, act_grad, preferred_element_type=jnp.float32)
    local_bias = jnp.sum(act_grad.astype(jnp.float32), axis=0)
    weight_grad, bias_grad = lax.psum((local_weight, local_bias), ("blk", "rep"))
    scale_factor = 1.0 / (blk_count * rep_count)
    weight_grad = weight_grad * scale_factor
    bias_grad = bias_grad * scale_factor
    agg_grad = jnp.dot(act_grad, weight.T, preferred_element_type=jnp.float32).astype(jnp.bfloat16)
    gathered = lax.all_gather(agg_grad, "rep", axis=0, tiled=True).reshape(
        rep_count * own_tiles, tile_size, feat_width
    )
    chosen = jnp.take(gathered, row_index, axis=0)
    contribution = (
        jnp.einsum("sij,sif->sjf", slot_tiles, chosen, preferred_element_type=jnp.float32)
        * slot_live[:, None, None]
    )

    def column_terms(first_row, row_count):
        targets = first_row // tile_size + jnp.arange(row_count // tile_size, dtype=jnp.int32)
        col_onehot = (col_index[:, None] == targets[None, :]).astype(jnp.float32)
        placed = jnp.einsum("sp,sjf->pjf", col_onehot, contribution, precision=highest)
        return placed.reshape(row_count, feat_width)

    own_block = lax.axis_index("blk")

    def travel_step(step_index, travelling):
        source_block = (own_block - step_index) % blk_count
        travelling = travelling + column_terms(source_block * own_rows, own_rows)
        return shifted(travelling, "blk", 1)

    feature_sum = lax.fori_loop(
        0, blk_count, travel_step, jnp.zeros((own_rows, feat_width), jnp.float32)
    )
    feature_grad = feature_sum.astype(jnp.bfloat16)
    return (activations, feature_grad, weight_grad, bias_grad)


def solution(mesh):
    in_specs = (
        P(("blk", "rep"), None),
        P("blk", "rep", None, None),
        P("blk", "rep"),
        P("blk", "rep"),
        P("blk", "rep"),
        P(),
        P(),
        P(("blk", "rep"), None),
    )
    out_specs = (P(("blk", "rep"), None), P(("blk", "rep"), None), P(), P())
    return jax.shard_map(
        per_device, mesh=mesh, in_specs=in_specs, out_specs=out_specs, check_vma=False
    )
```

profile of v0, /device:TPU:10, one launch (start us, length us, event | category | flops | bytes accessed | tf_op | source)
XLA Modules:
  0.0 242.8 jit_solution(17766153802447288838)
XLA Ops:
  9.5 40.9 %all-gather.2.cloned.1.call-done = bf16[2048,256]{1,0:T(8,128)(2,1)} async-done(((bf16[256,256]{1,0:T(8,128)(2,1)}), bf16[2048,256]{1,0:T(8,128)(2,1)}) %all-gather.2.cloned.1.call-update) | async-done | bytes 1048592 | tf_op jit(solution)/shard_map/all_gather | solution.py:27
  50.4 9.8 %gather_fusion = bf16[2048,256]{1,0:T(8,128)(2,1)} fusion(bf16[2048,256]{1,0:T(8,128)(2,1)} %all-gather.2.cloned.1.call-done, s32[2048]{0:T(1024)S(1)} %broadcast_clamp_fusion), kind=kCustom, calls=%fused_computation | custom fusion | bytes 2105344 | tf_op jit(solution)/shard_map/jit(_take)/gather | solution.py:31
  60.2 2.3 fusion.8
  62.6 2.1 copy.18
  64.7 2.7 %fusion.5 = f32[8,128,256]{2,0,1:T(8,128)S(1)} fusion(f32[16,256,128]{1,0,2:T(8,128)} %copy.18, f32[16]{0:T(128)S(1)} %compare_convert_fusion, s32[16]{0:T(128)S(1)} %bitcast.53), kind=kOutput, calls=%fused_computation.9 | convolution fusion | flops 50331904 | bytes 3145856 | tf_op jit(solution)/shard_map/st,sif->tif/dot_general | solution.py:39
  67.4 1.3 copy.15
  68.8 23.8 %reduce-scatter.2.cloned.1.call-done = f32[256,256]{1,0:T(8,128)} async-done(((f32[1024,256]{1,0:T(8,128)}), f32[256,256]{1,0:T(8,128)}) %reduce-scatter.2.cloned.1.call-update) | async-done | bytes 262160 | tf_op jit(solution)/shard_map/reduce_scatter | solution.py:40
  92.7 2.0 convert_reduce_fusion
  94.9 0.9 fusion.19
  95.8 7.2 %all_gather.7 = bf16[1024,256]{1,0:T(8,128)(2,1)S(1)} all-gather(bf16[256,256]{1,0:T(8,128)(2,1)S(1)} %convolution_convert_fusion), channel_id=1, replica_groups=mesh['blk'=8,'rep'=4] {'rep'}, dimensions={0}, use_global_device_ids=true | all-gather | bytes 655360 | tf_op jit(solution)/shard_map/all_gather | solution.py:56
  103.6 1.9 multiply_bitcast_fusion
  105.5 2.3 copy.17
  107.8 78.2 %while.15 = (s32[]{:T(128)}, f32[256,256]{1,0:T(8,128)S(1)}, s32[1,16]{1,0:T(1,128)S(1)}, s32[]{:T(128)}, f32[16,128,256]{2,0,1:T(8,128)S(1)}, /*index=5*/s32[]{...) while((s32[]{:T(128)}, f32[256,256]{1,0:T(8,128)S(1)}, ...), condition=%wide.region_2.3_spmd, body=%wide.region_1.2_spmd.sunk | while | flops 12648512 | bytes 4719116 | solution.py:78
  107.9 0.8 fusion.46
  108.8 1.5 collective-permute-start
  110.3 8.3 %collective-permute-done = f32[256,256]{1,0:T(8,128)S(1)} collective-permute-done((f32[256,256]{1,0:T(8,128)S(1)}, f32[256,256]{1,0:T(8,128)S(1)}, u32[]{:S(2)}, u32[]{:S(2)}) %collective-permute-start) | collective-permute-done | bytes 262176 | tf_op jit(solution)/shard_map/while/body/eval_jaxpr/ppermute | solution.py:10
  118.6 0.8 fusion.46
  120.0 8.6 %collective-permute-done = f32[256,256]{1,0:T(8,128)S(1)} collective-permute-done((f32[256,256]{1,0:T(8,128)S(1)}, f32[256,256]{1,0:T(8,128)S(1)}, u32[]{:S(2)}, u32[]{:S(2)}) %collective-permute-start) | collective-permute-done | bytes 262176 | tf_op jit(solution)/shard_map/while/body/eval_jaxpr/ppermute | solution.py:10
  128.5 0.8 fusion.46
  129.5 7.8 %collective-permute-done = f32[256,256]{1,0:T(8,128)S(1)} collective-permute-done((f32[256,256]{1,0:T(8,128)S(1)}, f32[256,256]{1,0:T(8,128)S(1)}, u32[]{:S(2)}, u32[]{:S(2)}) %collective-permute-start) | collective-permute-done | bytes 262176 | tf_op jit(solution)/shard_map/while/body/eval_jaxpr/ppermute | solution.py:10
  137.3 0.8 fusion.46
  138.3 7.8 %collective-permute-done = f32[256,256]{1,0:T(8,128)S(1)} collective-permute-done((f32[256,256]{1,0:T(8,128)S(1)}, f32[256,256]{1,0:T(8,128)S(1)}, u32[]{:S(2)}, u32[]{:S(2)}) %collective-permute-start) | collective-permute-done | bytes 262176 | tf_op jit(solution)/shard_map/while/body/eval_jaxpr/ppermute | solution.py:10
  146.1 0.8 fusion.46
  147.1 8.3 %collective-permute-done = f32[256,256]{1,0:T(8,128)S(1)} collective-permute-done((f32[256,256]{1,0:T(8,128)S(1)}, f32[256,256]{1,0:T(8,128)S(1)}, u32[]{:S(2)}, u32[]{:S(2)}) %collective-permute-start) | collective-permute-done | bytes 262176 | tf_op jit(solution)/shard_map/while/body/eval_jaxpr/ppermute | solution.py:10
  155.4 0.8 fusion.46
  156.4 9.1 %collective-permute-done = f32[256,256]{1,0:T(8,128)S(1)} collective-permute-done((f32[256,256]{1,0:T(8,128)S(1)}, f32[256,256]{1,0:T(8,128)S(1)}, u32[]{:S(2)}, u32[]{:S(2)}) %collective-permute-start) | collective-permute-done | bytes 262176 | tf_op jit(solution)/shard_map/while/body/eval_jaxpr/ppermute | solution.py:10
  165.5 0.8 fusion.46
  166.5 9.4 %collective-permute-done = f32[256,256]{1,0:T(8,128)S(1)} collective-permute-done((f32[256,256]{1,0:T(8,128)S(1)}, f32[256,256]{1,0:T(8,128)S(1)}, u32[]{:S(2)}, u32[]{:S(2)}) %collective-permute-start) | collective-permute-done | bytes 262176 | tf_op jit(solution)/shard_map/while/body/eval_jaxpr/ppermute | solution.py:10
  175.9 0.8 fusion.46
  176.8 9.1 %collective-permute-done = f32[256,256]{1,0:T(8,128)S(1)} collective-permute-done((f32[256,256]{1,0:T(8,128)S(1)}, f32[256,256]{1,0:T(8,128)S(1)}, u32[]{:S(2)}, u32[]{:S(2)}) %collective-permute-start) | collective-permute-done | bytes 262176 | tf_op jit(solution)/shard_map/while/body/eval_jaxpr/ppermute | solution.py:10
  186.7 47.3 %psum.15 = f32[256]{0:T(256)S(1)} all-reduce(f32[256]{0:T(256)S(1)} %get-tuple-element.160), channel_id=1, replica_groups=mesh['blk'=8,'rep'=4] {'blk','rep'}, use_global_device_ids=true, to_apply=%region_5.6 | all-reduce | flops 256 | bytes 2048 | tf_op jit(solution)/shard_map/psum | solution.py:51
  234.6 1.7 broadcast_multiply_fusion
  (66 shorter events, 5.1 us)
Async XLA Ops:
  7.2 53.1 %copy-start = (bf16[1,16,128,128]{3,2,1,0:T(8,128)(2,1)S(1)}, bf16[1,16,128,128]{3,2,1,0:T(8,128)(2,1)}, u32[]{:S(2)}) copy-start(bf16[1,16,128,128]{3,2,1,0:T(8,128)(2,1)} %param.11) | copy-start | bytes 1572868
  7.2 43.2 %all-gather.2.cloned.1.call-start = ((), (), s32[]{:S(2)}) async-start(), calls=%async_computation.1 | async-start | bytes 1179648 | tf_op jit(solution)/shard_map/all_gather | solution.py:27
  7.9 84.7 %reduce-scatter.2.cloned.1.call-start = ((), (), s32[]{:S(2)}) async-start(), calls=%async_computation.2 | async-start | bytes 1310720 | tf_op jit(solution)/shard_map/reduce_scatter | solution.py:40
  62.6 2.1 copy-start.4
  67.4 25.3 %copy-start.2 = (bf16[256,256]{1,0:T(8,128)(2,1)S(1)}, bf16[256,256]{1,0:T(8,128)(2,1)}, u32[]{:S(2)}) copy-start(bf16[256,256]{1,0:T(8,128)(2,1)} %param.15) | copy-start | bytes 393220
  67.4 25.3 %copy-start.5 = (bf16[256,256]{1,0:T(8,128)(2,1)S(1)}, bf16[256,256]{1,0:T(8,128)(2,1)}, u32[]{:S(2)}) copy-start(bf16[256,256]{1,0:T(8,128)(2,1)} %param.17) | copy-start | bytes 393220
  67.4 25.2 %copy-start.6 = (f32[256]{0:T(256)S(1)}, f32[256]{0:T(256)}, u32[]{:S(2)}) copy-start(f32[256]{0:T(256)} %param.16) | copy-start | bytes 3076
  68.7 165.8 %all-reduce.2.cloned.1.call-start = ((), (), s32[]{:S(2)}) async-start(), calls=%async_computation.3 | async-start | bytes 524288 | tf_op jit(solution)/shard_map/psum | solution.py:51
  92.6 2.2 copy-start.1
  105.5 2.3 copy-start.3
  108.8 9.8 %collective-permute-start = (f32[256,256]{1,0:T(8,128)S(1)}, f32[256,256]{1,0:T(8,128)S(1)}, u32[]{:S(2)}, u32[]{:S(2)}) collective-permute-start(f32[256,256]{1,0:T(8,128)S(1)} %bitcast_add_fusion.2), channel_id=1, source_target_pairs={{28,0},{0,4},{4,8},{8,12},{12,16},{16,20},{20,24},{24,28},{29,1},{... | collective-permute-start | bytes 786440 | tf_op jit(solution)/shard_map/while/body/eval_jaxpr/ppermute | solution.py:10
  119.5 9.0 %collective-permute-start = (f32[256,256]{1,0:T(8,128)S(1)}, f32[256,256]{1,0:T(8,128)S(1)}, u32[]{:S(2)}, u32[]{:S(2)}) collective-permute-start(f32[256,256]{1,0:T(8,128)S(1)} %bitcast_add_fusion.2), channel_id=1, source_target_pairs={{28,0},{0,4},{4,8},{8,12},{12,16},{16,20},{20,24},{24,28},{29,1},{... | collective-permute-start | bytes 786440 | tf_op jit(solution)/shard_map/while/body/eval_jaxpr/ppermute | solution.py:10
  129.4 7.9 %collective-permute-start = (f32[256,256]{1,0:T(8,128)S(1)}, f32[256,256]{1,0:T(8,128)S(1)}, u32[]{:S(2)}, u32[]{:S(2)}) collective-permute-start(f32[256,256]{1,0:T(8,128)S(1)} %bitcast_add_fusion.2), channel_id=1, source_target_pairs={{28,0},{0,4},{4,8},{8,12},{12,16},{16,20},{20,24},{24,28},{29,1},{... | collective-permute-start | bytes 786440 | tf_op jit(solution)/shard_map/while/body/eval_jaxpr/ppermute | solution.py:10
  138.2 7.9 %collective-permute-start = (f32[256,256]{1,0:T(8,128)S(1)}, f32[256,256]{1,0:T(8,128)S(1)}, u32[]{:S(2)}, u32[]{:S(2)}) collective-permute-start(f32[256,256]{1,0:T(8,128)S(1)} %bitcast_add_fusion.2), channel_id=1, source_target_pairs={{28,0},{0,4},{4,8},{8,12},{12,16},{16,20},{20,24},{24,28},{29,1},{... | collective-permute-start | bytes 786440 | tf_op jit(solution)/shard_map/while/body/eval_jaxpr/ppermute | solution.py:10
  147.0 8.4 %collective-permute-start = (f32[256,256]{1,0:T(8,128)S(1)}, f32[256,256]{1,0:T(8,128)S(1)}, u32[]{:S(2)}, u32[]{:S(2)}) collective-permute-start(f32[256,256]{1,0:T(8,128)S(1)} %bitcast_add_fusion.2), channel_id=1, source_target_pairs={{28,0},{0,4},{4,8},{8,12},{12,16},{16,20},{20,24},{24,28},{29,1},{... | collective-permute-start | bytes 786440 | tf_op jit(solution)/shard_map/while/body/eval_jaxpr/ppermute | solution.py:10
  156.3 9.2 %collective-permute-start = (f32[256,256]{1,0:T(8,128)S(1)}, f32[256,256]{1,0:T(8,128)S(1)}, u32[]{:S(2)}, u32[]{:S(2)}) collective-permute-start(f32[256,256]{1,0:T(8,128)S(1)} %bitcast_add_fusion.2), channel_id=1, source_target_pairs={{28,0},{0,4},{4,8},{8,12},{12,16},{16,20},{20,24},{24,28},{29,1},{... | collective-permute-start | bytes 786440 | tf_op jit(solution)/shard_map/while/body/eval_jaxpr/ppermute | solution.py:10
  166.4 9.5 %collective-permute-start = (f32[256,256]{1,0:T(8,128)S(1)}, f32[256,256]{1,0:T(8,128)S(1)}, u32[]{:S(2)}, u32[]{:S(2)}) collective-permute-start(f32[256,256]{1,0:T(8,128)S(1)} %bitcast_add_fusion.2), channel_id=1, source_target_pairs={{28,0},{0,4},{4,8},{8,12},{12,16},{16,20},{20,24},{24,28},{29,1},{... | collective-permute-start | bytes 786440 | tf_op jit(solution)/shard_map/while/body/eval_jaxpr/ppermute | solution.py:10
  176.8 9.2 %collective-permute-start = (f32[256,256]{1,0:T(8,128)S(1)}, f32[256,256]{1,0:T(8,128)S(1)}, u32[]{:S(2)}, u32[]{:S(2)}) collective-permute-start(f32[256,256]{1,0:T(8,128)S(1)} %bitcast_add_fusion.2), channel_id=1, source_target_pairs={{28,0},{0,4},{4,8},{8,12},{12,16},{16,20},{20,24},{24,28},{29,1},{... | collective-permute-start | bytes 786440 | tf_op jit(solution)/shard_map/while/body/eval_jaxpr/ppermute | solution.py:10
Sparse Core Ops, SparseCore 0:
  10.1 40.2 all-gather.1
  68.9 23.7 reduce-scatter.1
  98.7 131.8 all-reduce.1
where the time goes:
time: 243 us
  waiting for transfers between devices  134 us (55%)
  blocking collectives  54.5 us (22%)
  matrix products  16.7 us (7%)
  local copies, waits for them, and re-layouts  16.3 us (7%)
  between operations  14.6 us (6%)
  other arithmetic  4.1 us (2%)
  starting transfers between devices  2.45 us (1%)
    ppermute x8, waiting for transfers between devices, shifted(): return lax.ppermute(block, axis, route)  68.5 us
    psum x1, blocking collectives, per_device(): lax.psum((local_weight, local_bias), ('blk', 'rep'))  47.3 us
    all_gather x1, waiting for transfers between devices, per_device(): piece = lax.all_gather(features, 'blk', axis=0, tiled=True)  40.9 us
    reduce_scatter x1, waiting for transfers between devices, per_device(): lax.psum_scatter(summed.reshape(rep_count * own_rows, feat_width), 'rep',...  23.8 us
    gather x1, local copies, waits for them, and re-layouts, per_device(): jnp.take(piece, clipped.reshape(-1), axis=0)  9.83 us
    all_gather x1, blocking collectives, per_device(): lax.all_gather(agg_grad, 'rep', axis=0, tiled=True)  7.17 us
    dot_general x8, matrix products, column_terms(): jnp.einsum('sp,sjf->pjf', col_onehot, contribution, precision=highest)  6.58 us
  transfers between devices with their start and end apart: 11, of which 10 were waited for; matrix products, arithmetic and copies ran while one was open for 6% of the time, Pallas kernels for 0%

commit v1 on v0

--- a/solution.py
+++ b/solution.py
@@ -1,7 +1,17 @@
+import functools
 import jax
 import jax.numpy as jnp
 from jax import lax
 from jax.sharding import PartitionSpec as P
+
+
+def _touch_task(values, bus_axis, axis_id):
+    for nth in (bus_axis, axis_id):
+        values = lax.psum(values, nth)
+    return values
+
+
+_turn_counts = functools.partial(_touch_task, bus_axis="blk", axis_id="rep")
 
 
 def shifted(block, axis, distance):
@@ -48,7 +58,7 @@
     ).astype(jnp.bfloat16)
     local_weight = jnp.dot(aggregate.T, act_grad, preferred_element_type=jnp.float32)
     local_bias = jnp.sum(act_grad.astype(jnp.float32), axis=0)
-    weight_grad, bias_grad = lax.psum((local_weight, local_bias), ("blk", "rep"))
+    weight_grad, bias_grad = _turn_counts((local_weight, local_bias))
     scale_factor = 1.0 / (blk_count * rep_count)
     weight_grad = weight_grad * scale_factor
     bias_grad = bias_grad * scale_factor

time: 243 us -> 259 us (1.066)
  waiting for transfers between devices: 134 us -> 168 us
  blocking collectives: 54.5 us -> 34.7 us
    psum x1 -> x2, waiting for transfers between devices: 0.01 us -> 32.2 us  [_touch_task(): values = lax.psum(values, nth)]
    psum x1 -> x2, blocking collectives: 47.3 us -> 27.5 us  [_touch_task(): values = lax.psum(values, nth)]
  transfers between devices with their start and end apart: 11 -> 12, of which waited for: 10 -> 11; matrix products, arithmetic and copies ran while one was open for 6% -> 5% of each run, Pallas kernels for 0% -> 0%
where the time goes in v1:
time: 259 us; the launch traced here: 256 us
  waiting for transfers between devices  168 us (65%)
  blocking collectives  34.7 us (13%)
  matrix products  16.7 us (6%)
  local copies, waits for them, and re-layouts  16.2 us (6%)
  between operations  14.6 us (6%)
  other arithmetic  4.1 us (2%)
    ppermute x8, waiting for transfers between devices, shifted(): return lax.ppermute(block, axis, route)  70 us
    all_gather x1, waiting for transfers between devices, per_device(): piece = lax.all_gather(features, 'blk', axis=0, tiled=True)  40.9 us
    psum x2, waiting for transfers between devices, _touch_task(): values = lax.psum(values, nth)  32.2 us
    psum x2, blocking collectives, _touch_task(): values = lax.psum(values, nth)  27.5 us
    reduce_scatter x1, waiting for transfers between devices, per_device(): lax.psum_scatter(summed.reshape(rep_count * own_rows, feat_width), 'rep',...  23.8 us
    gather x1, local copies, waits for them, and re-layouts, per_device(): jnp.take(piece, clipped.reshape(-1), axis=0)  9.81 us
    all_gather x1, blocking collectives, per_device(): lax.all_gather(agg_grad, 'rep', axis=0, tiled=True)  7.16 us
    dot_general x8, matrix products, column_terms(): jnp.einsum('sp,sjf->pjf', col_onehot, contribution, precision=highest)  6.57 us
  transfers between devices with their start and end apart: 12, of which 11 were waited for; matrix products, arithmetic and copies ran while one was open for 5% of the time, Pallas kernels for 0%

profile of v1, /device:TPU:10, one launch (start us, length us, event | category | flops | bytes accessed | tf_op | source)
XLA Modules:
  0.0 256.3 jit_solution(17470063217702196965)
XLA Ops:
  9.5 40.9 %all-gather.2.cloned.1.call-done = bf16[2048,256]{1,0:T(8,128)(2,1)} async-done(((bf16[256,256]{1,0:T(8,128)(2,1)}), bf16[2048,256]{1,0:T(8,128)(2,1)}) %all-gather.2.cloned.1.call-update) | async-done | bytes 1048592 | tf_op jit(solution)/shard_map/all_gather | solution.py:37
  50.4 9.8 %gather_fusion = bf16[2048,256]{1,0:T(8,128)(2,1)} fusion(bf16[2048,256]{1,0:T(8,128)(2,1)} %all-gather.2.cloned.1.call-done, s32[2048]{0:T(1024)S(1)} %broadcast_clamp_fusion), kind=kCustom, calls=%fused_computation | custom fusion | bytes 2105344 | tf_op jit(solution)/shard_map/jit(_take)/gather | solution.py:41
  60.2 2.3 fusion.8
  62.6 2.1 copy.18
  64.6 2.7 %fusion.5 = f32[8,128,256]{2,0,1:T(8,128)S(1)} fusion(f32[16,256,128]{1,0,2:T(8,128)} %copy.18, f32[16]{0:T(128)S(1)} %compare_convert_fusion, s32[16]{0:T(128)S(1)} %bitcast.53), kind=kOutput, calls=%fused_computation.9 | convolution fusion | flops 50331904 | bytes 3145856 | tf_op jit(solution)/shard_map/st,sif->tif/dot_general | solution.py:49
  67.4 1.3 copy.15
  68.8 23.8 %reduce-scatter.2.cloned.1.call-done = f32[256,256]{1,0:T(8,128)} async-done(((f32[1024,256]{1,0:T(8,128)}), f32[256,256]{1,0:T(8,128)}) %reduce-scatter.2.cloned.1.call-update) | async-done | bytes 262160 | tf_op jit(solution)/shard_map/reduce_scatter | solution.py:50
  92.6 2.0 convert_reduce_fusion
  94.8 0.9 fusion.19
  95.8 7.2 %all_gather.7 = bf16[1024,256]{1,0:T(8,128)(2,1)S(1)} all-gather(bf16[256,256]{1,0:T(8,128)(2,1)S(1)} %convolution_convert_fusion), channel_id=1, replica_groups=mesh['blk'=8,'rep'=4] {'rep'}, dimensions={0}, use_global_device_ids=true | all-gather | bytes 655360 | tf_op jit(solution)/shard_map/all_gather | solution.py:66
  103.6 1.9 multiply_bitcast_fusion
  105.5 2.2 copy.17
  107.8 79.3 %while.15 = (s32[]{:T(128)}, f32[256,256]{1,0:T(8,128)S(1)}, s32[1,16]{1,0:T(1,128)S(1)}, s32[]{:T(128)}, f32[16,128,256]{2,0,1:T(8,128)S(1)}, /*index=5*/s32[]{...) while((s32[]{:T(128)}, f32[256,256]{1,0:T(8,128)S(1)}, ...), condition=%wide.region_2.3_spmd, body=%wide.region_1.2_spmd.sunk | while | flops 12648512 | bytes 4719116 | solution.py:88
  108.8 1.5 collective-permute-start
  110.3 8.5 %collective-permute-done = f32[256,256]{1,0:T(8,128)S(1)} collective-permute-done((f32[256,256]{1,0:T(8,128)S(1)}, f32[256,256]{1,0:T(8,128)S(1)}, u32[]{:S(2)}, u32[]{:S(2)}) %collective-permute-start) | collective-permute-done | bytes 262176 | tf_op jit(solution)/shard_map/while/body/eval_jaxpr/ppermute | solution.py:20
  118.8 0.8 fusion.46
  119.8 9.3 %collective-permute-done = f32[256,256]{1,0:T(8,128)S(1)} collective-permute-done((f32[256,256]{1,0:T(8,128)S(1)}, f32[256,256]{1,0:T(8,128)S(1)}, u32[]{:S(2)}, u32[]{:S(2)}) %collective-permute-start) | collective-permute-done | bytes 262176 | tf_op jit(solution)/shard_map/while/body/eval_jaxpr/ppermute | solution.py:20
  129.1 0.8 fusion.46
  130.0 7.7 %collective-permute-done = f32[256,256]{1,0:T(8,128)S(1)} collective-permute-done((f32[256,256]{1,0:T(8,128)S(1)}, f32[256,256]{1,0:T(8,128)S(1)}, u32[]{:S(2)}, u32[]{:S(2)}) %collective-permute-start) | collective-permute-done | bytes 262176 | tf_op jit(solution)/shard_map/while/body/eval_jaxpr/ppermute | solution.py:20
  137.8 0.8 fusion.46
  138.8 8.4 %collective-permute-done = f32[256,256]{1,0:T(8,128)S(1)} collective-permute-done((f32[256,256]{1,0:T(8,128)S(1)}, f32[256,256]{1,0:T(8,128)S(1)}, u32[]{:S(2)}, u32[]{:S(2)}) %collective-permute-start) | collective-permute-done | bytes 262176 | tf_op jit(solution)/shard_map/while/body/eval_jaxpr/ppermute | solution.py:20
  148.1 8.0 %collective-permute-done = f32[256,256]{1,0:T(8,128)S(1)} collective-permute-done((f32[256,256]{1,0:T(8,128)S(1)}, f32[256,256]{1,0:T(8,128)S(1)}, u32[]{:S(2)}, u32[]{:S(2)}) %collective-permute-start) | collective-permute-done | bytes 262176 | tf_op jit(solution)/shard_map/while/body/eval_jaxpr/ppermute | solution.py:20
  156.2 0.8 fusion.46
  157.1 10.2 %collective-permute-done = f32[256,256]{1,0:T(8,128)S(1)} collective-permute-done((f32[256,256]{1,0:T(8,128)S(1)}, f32[256,256]{1,0:T(8,128)S(1)}, u32[]{:S(2)}, u32[]{:S(2)}) %collective-permute-start) | collective-permute-done | bytes 262176 | tf_op jit(solution)/shard_map/while/body/eval_jaxpr/ppermute | solution.py:20
  167.3 0.8 fusion.46
  168.3 8.3 %collective-permute-done = f32[256,256]{1,0:T(8,128)S(1)} collective-permute-done((f32[256,256]{1,0:T(8,128)S(1)}, f32[256,256]{1,0:T(8,128)S(1)}, u32[]{:S(2)}, u32[]{:S(2)}) %collective-permute-start) | collective-permute-done | bytes 262176 | tf_op jit(solution)/shard_map/while/body/eval_jaxpr/ppermute | solution.py:20
  176.5 0.8 fusion.46
  177.5 9.6 %collective-permute-done = f32[256,256]{1,0:T(8,128)S(1)} collective-permute-done((f32[256,256]{1,0:T(8,128)S(1)}, f32[256,256]{1,0:T(8,128)S(1)}, u32[]{:S(2)}, u32[]{:S(2)}) %collective-permute-start) | collective-permute-done | bytes 262176 | tf_op jit(solution)/shard_map/while/body/eval_jaxpr/ppermute | solution.py:20
  187.8 21.9 %psum.30 = f32[256]{0:T(256)S(1)} all-reduce(f32[256]{0:T(256)S(1)} %get-tuple-element.160), channel_id=1, replica_groups=mesh['blk'=8,'rep'=4] {'blk'}, use_global_device_ids=true, to_apply=%region_6.7 | all-reduce | flops 256 | bytes 2048 | tf_op jit(solution)/shard_map/psum | solution.py:10
  209.7 5.7 %psum.31 = f32[256]{0:T(256)S(1)} all-reduce(f32[256]{0:T(256)S(1)} %psum.30), channel_id=1, replica_groups=mesh['blk'=8,'rep'=4] {'rep'}, use_global_device_ids=true, to_apply=%region_7.8 | all-reduce | flops 256 | bytes 2048 | tf_op jit(solution)/shard_map/psum | solution.py:10
  215.9 32.2 %all-reduce.5.cloned.1.call-done = f32[256,256]{1,0:T(8,128)} async-done(((f32[256,256]{1,0:T(8,128)}), f32[256,256]{1,0:T(8,128)}) %all-reduce.5.cloned.1.call-update) | async-done | bytes 262160 | tf_op jit(solution)/shard_map/psum | solution.py:10
  248.1 1.7 broadcast_multiply_fusion
  (70 shorter events, 6.5 us)
Async XLA Ops:
  7.2 53.1 %copy-start = (bf16[1,16,128,128]{3,2,1,0:T(8,128)(2,1)S(1)}, bf16[1,16,128,128]{3,2,1,0:T(8,128)(2,1)}, u32[]{:S(2)}) copy-start(bf16[1,16,128,128]{3,2,1,0:T(8,128)(2,1)} %param.11) | copy-start | bytes 1572868
  7.2 43.2 %all-gather.2.cloned.1.call-start = ((), (), s32[]{:S(2)}) async-start(), calls=%async_computation.1 | async-start | bytes 1179648 | tf_op jit(solution)/shard_map/all_gather | solution.py:37
  7.9 84.7 %reduce-scatter.2.cloned.1.call-start = ((), (), s32[]{:S(2)}) async-start(), calls=%async_computation.2 | async-start | bytes 1310720 | tf_op jit(solution)/shard_map/reduce_scatter | solution.py:50
  62.6 2.1 copy-start.4
  67.4 25.2 %copy-start.2 = (bf16[256,256]{1,0:T(8,128)(2,1)S(1)}, bf16[256,256]{1,0:T(8,128)(2,1)}, u32[]{:S(2)}) copy-start(bf16[256,256]{1,0:T(8,128)(2,1)} %param.15) | copy-start | bytes 393220
  67.4 25.2 %copy-start.5 = (bf16[256,256]{1,0:T(8,128)(2,1)S(1)}, bf16[256,256]{1,0:T(8,128)(2,1)}, u32[]{:S(2)}) copy-start(bf16[256,256]{1,0:T(8,128)(2,1)} %param.17) | copy-start | bytes 393220
  67.4 25.2 %copy-start.6 = (f32[256]{0:T(256)S(1)}, f32[256]{0:T(256)}, u32[]{:S(2)}) copy-start(f32[256]{0:T(256)} %param.16) | copy-start | bytes 3076
  68.7 146.6 %all-reduce.3.cloned.1.call-start = ((), (), s32[]{:S(2)}) async-start(), calls=%async_computation.3 | async-start | bytes 524288 | tf_op jit(solution)/shard_map/psum | solution.py:10
  92.6 2.2 copy-start.1
  95.8 152.4 %all-reduce.5.cloned.1.call-start = ((), (), s32[]{:S(2)}) async-start(), calls=%async_computation.4 | async-start | bytes 524288 | tf_op jit(solution)/shard_map/psum | solution.py:10
  105.5 2.3 copy-start.3
  108.8 10.0 %collective-permute-start = (f32[256,256]{1,0:T(8,128)S(1)}, f32[256,256]{1,0:T(8,128)S(1)}, u32[]{:S(2)}, u32[]{:S(2)}) collective-permute-start(f32[256,256]{1,0:T(8,128)S(1)} %bitcast_add_fusion.2), channel_id=1, source_target_pairs={{28,0},{0,4},{4,8},{8,12},{12,16},{16,20},{20,24},{24,28},{29,1},{... | collective-permute-start | bytes 786440 | tf_op jit(solution)/shard_map/while/body/eval_jaxpr/ppermute | solution.py:20
  119.7 9.4 %collective-permute-start = (f32[256,256]{1,0:T(8,128)S(1)}, f32[256,256]{1,0:T(8,128)S(1)}, u32[]{:S(2)}, u32[]{:S(2)}) collective-permute-start(f32[256,256]{1,0:T(8,128)S(1)} %bitcast_add_fusion.2), channel_id=1, source_target_pairs={{28,0},{0,4},{4,8},{8,12},{12,16},{16,20},{20,24},{24,28},{29,1},{... | collective-permute-start | bytes 786440 | tf_op jit(solution)/shard_map/while/body/eval_jaxpr/ppermute | solution.py:20
  130.0 7.8 %collective-permute-start = (f32[256,256]{1,0:T(8,128)S(1)}, f32[256,256]{1,0:T(8,128)S(1)}, u32[]{:S(2)}, u32[]{:S(2)}) collective-permute-start(f32[256,256]{1,0:T(8,128)S(1)} %bitcast_add_fusion.2), channel_id=1, source_target_pairs={{28,0},{0,4},{4,8},{8,12},{12,16},{16,20},{20,24},{24,28},{29,1},{... | collective-permute-start | bytes 786440 | tf_op jit(solution)/shard_map/while/body/eval_jaxpr/ppermute | solution.py:20
  138.7 8.4 %collective-permute-start = (f32[256,256]{1,0:T(8,128)S(1)}, f32[256,256]{1,0:T(8,128)S(1)}, u32[]{:S(2)}, u32[]{:S(2)}) collective-permute-start(f32[256,256]{1,0:T(8,128)S(1)} %bitcast_add_fusion.2), channel_id=1, source_target_pairs={{28,0},{0,4},{4,8},{8,12},{12,16},{16,20},{20,24},{24,28},{29,1},{... | collective-permute-start | bytes 786440 | tf_op jit(solution)/shard_map/while/body/eval_jaxpr/ppermute | solution.py:20
  148.0 8.1 %collective-permute-start = (f32[256,256]{1,0:T(8,128)S(1)}, f32[256,256]{1,0:T(8,128)S(1)}, u32[]{:S(2)}, u32[]{:S(2)}) collective-permute-start(f32[256,256]{1,0:T(8,128)S(1)} %bitcast_add_fusion.2), channel_id=1, source_target_pairs={{28,0},{0,4},{4,8},{8,12},{12,16},{16,20},{20,24},{24,28},{29,1},{... | collective-permute-start | bytes 786440 | tf_op jit(solution)/shard_map/while/body/eval_jaxpr/ppermute | solution.py:20
  157.1 10.3 %collective-permute-start = (f32[256,256]{1,0:T(8,128)S(1)}, f32[256,256]{1,0:T(8,128)S(1)}, u32[]{:S(2)}, u32[]{:S(2)}) collective-permute-start(f32[256,256]{1,0:T(8,128)S(1)} %bitcast_add_fusion.2), channel_id=1, source_target_pairs={{28,0},{0,4},{4,8},{8,12},{12,16},{16,20},{20,24},{24,28},{29,1},{... | collective-permute-start | bytes 786440 | tf_op jit(solution)/shard_map/while/body/eval_jaxpr/ppermute | solution.py:20
  168.2 8.3 %collective-permute-start = (f32[256,256]{1,0:T(8,128)S(1)}, f32[256,256]{1,0:T(8,128)S(1)}, u32[]{:S(2)}, u32[]{:S(2)}) collective-permute-start(f32[256,256]{1,0:T(8,128)S(1)} %bitcast_add_fusion.2), channel_id=1, source_target_pairs={{28,0},{0,4},{4,8},{8,12},{12,16},{16,20},{20,24},{24,28},{29,1},{... | collective-permute-start | bytes 786440 | tf_op jit(solution)/shard_map/while/body/eval_jaxpr/ppermute | solution.py:20
  177.4 9.7 %collective-permute-start = (f32[256,256]{1,0:T(8,128)S(1)}, f32[256,256]{1,0:T(8,128)S(1)}, u32[]{:S(2)}, u32[]{:S(2)}) collective-permute-start(f32[256,256]{1,0:T(8,128)S(1)} %bitcast_add_fusion.2), channel_id=1, source_target_pairs={{28,0},{0,4},{4,8},{8,12},{12,16},{16,20},{20,24},{24,28},{29,1},{... | collective-permute-start | bytes 786440 | tf_op jit(solution)/shard_map/while/body/eval_jaxpr/ppermute | solution.py:20
Sparse Core Ops, SparseCore 0:
  10.1 40.2 all-gather.1
  68.8 23.7 reduce-scatter.1
  96.5 75.0 all-reduce.2
  215.5 32.6 all-reduce.4
